TPU v7x, 32 devices: a whole 2x2x4 slice. The times are simulated.
32 devices in a mesh: ob: 8 (over z, core), pt: 4 (over y, x).
Axes of the slice: x: 2, y: 2, z: 4, core: 2. Of those that a mesh axis runs over, the one named last changes fastest.
Arguments:
- orbitals: float32 [128, 262144], P(('ob', 'pt')), may hold values from -32 to 32, as said below
- potential: float32 [262144], replicated, may hold values from 0 to 2
- cutoff: float32 [1], replicated, may hold values from 0.4 to 1
- eigvec: float32 [128, 128], replicated, may hold values from -3 to 3, as said below
Outputs:
- gram: float32 [128, 128], P(('ob', 'pt'))
- hamil_sub: float32 [128, 128], P(('ob', 'pt'))
- rotated: float32 [128, 262144], P(None, ('ob', 'pt'))
- residual: float32 [128, 262144], P(None, ('ob', 'pt'))
- ritz: float32 [128], replicated
Inputs may be any that keep to these rules, and one draw needn't show every extreme that they name: `orbitals`: each orbital is a rough field whose scale differs from orbital to orbital and from region to region of the grid. `eigvec`: A full-rank matrix with a unit-sized diagonal and independent off-diagonal entries.
All inputs are finite; a program needn't handle non-finite values.
Results may differ from a plain program's by a relative error of at most 0.00027.
Values sent between devices are 32-bit elements; how exact they have to be, the bound alone decides.
A program may use at most 128 MiB of HBM per device.

v0:
```python
import jax
import jax.numpy as jnp
from jax import lax
from jax.sharding import PartitionSpec as P

G = 64
DEGREE = 12
NPTS = 262144
upper_bound = 8.0
quot_eps = 1e-06


def apply_ham(fields, potential):
    points = fields.shape[-1]
    plane_len = G * G
    x_pair = jnp.roll(fields, plane_len, axis=-1) + jnp.roll(fields, -plane_len, axis=-1)
    cube_view = fields.reshape(fields.shape[0], G, plane_len)
    y_pair = (jnp.roll(cube_view, G, axis=-1) + jnp.roll(cube_view, -G, axis=-1)).reshape(
        fields.shape
    )
    z_index = lax.broadcasted_iota(jnp.int32, (1, points), 1) % G
    z_lower = jnp.where(
        z_index == 0, jnp.roll(fields, 1 - G, axis=-1), jnp.roll(fields, 1, axis=-1)
    )
    z_upper = jnp.where(
        z_index == G - 1, jnp.roll(fields, G - 1, axis=-1), jnp.roll(fields, -1, axis=-1)
    )
    return -0.5 * (x_pair + y_pair + z_lower + z_upper - 6.0 * fields) + potential * fields


def chebyshev(fields, potential, cutoff):
    center = 0.5 * (upper_bound + cutoff[0])
    half_width = 0.5 * (upper_bound - cutoff[0])
    current = (apply_ham(fields, potential) - center * fields) / half_width

    def advance(turn_idx, carry):
        previous, present = carry
        following = 2.0 * (apply_ham(present, potential) - center * present) / half_width - previous
        return (present, following)

    previous, current = lax.fori_loop(0, DEGREE - 1, advance, (fields, current))
    return (current, apply_ham(current, potential))


def on_device(orbitals, potential, cutoff, eigvec):
    high = lax.Precision.HIGHEST
    filtered, applied = chebyshev(orbitals, potential, cutoff)
    total_orb = eigvec.shape[0]
    n_ob = lax.axis_size("ob")
    n_pt = lax.axis_size("pt")
    per_dev = total_orb // (n_ob * n_pt)
    rows_filt, rows_appl = (
        lax.all_to_all(filtered, ("ob", "pt"), split_axis=1, concat_axis=0, tiled=True),
        lax.all_to_all(applied, ("ob", "pt"), split_axis=1, concat_axis=0, tiled=True),
    )
    part_gram = jnp.dot(rows_filt, rows_filt.T, precision=high) / NPTS
    part_hamil = jnp.dot(rows_filt, rows_appl.T, precision=high) / NPTS
    gram, hamil_sub = (
        lax.psum_scatter(part_gram, ("ob", "pt"), scatter_dimension=0, tiled=True),
        lax.psum_scatter(part_hamil, ("ob", "pt"), scatter_dimension=0, tiled=True),
    )
    rotated = jnp.dot(eigvec.T, rows_filt, precision=high)
    rot_applied = jnp.dot(eigvec.T, rows_appl, precision=high)
    my_index = lax.axis_index(("ob", "pt"))
    my_rows = lax.dynamic_slice_in_dim(eigvec, my_index * per_dev, per_dev, 0)
    numer = jnp.sum(my_rows * jnp.dot(hamil_sub, eigvec, precision=high), axis=0)
    denom = jnp.sum(my_rows * jnp.dot(gram, eigvec, precision=high), axis=0)
    numer, denom = lax.psum((numer, denom), ("ob", "pt"))
    ritz = numer / (denom + quot_eps)
    residual = rot_applied - ritz[:, None] * rotated
    return (gram, hamil_sub, rotated, residual, ritz)


def solution(mesh):
    return jax.shard_map(
        on_device,
        mesh=mesh,
        in_specs=(P(("ob", "pt"), None), P(), P(), P()),
        out_specs=(
            P(("ob", "pt"), None),
            P(("ob", "pt"), None),
            P(None, ("ob", "pt")),
            P(None, ("ob", "pt")),
            P(),
        ),
        check_vma=False,
    )
```

profile of v0, /device:TPU:0, one launch (start us, length us, event | category | flops | bytes accessed | tf_op | source)
XLA Modules:
  0.0 1040.0 jit_solution(13240792252912524412)
XLA Ops:
  13.5 4.6 fusion.57
  18.1 4.5 fusion.60
  28.6 4.7 copy.22
  33.3 24.7 %fusion.29 = f32[4,262144]{1,0:T(4,128)} fusion(f32[4,262144]{1,0:T(4,128)} %copy-done.2, f32[4,1]{1,0:T(4,128)S(1)} %get-tuple-element.162, f32[4,262143]{1,0:T(4,128)} %get-tuple-element.164, f32[4,262081]{1,0:T(4,128)} %get-tuple-element.158, f32[4,63]{1,0:T(4,128)S(1)} %get-tuple-element.160, f32[4,262143]{1,0:T(4,128)} %get-tuple-element.163, ...), kind=kLoop, calls=%fused_computation.49 | loop fusion | flops 20971520 | bytes 39321608 | tf_op jit(solution)/shard_map/div | solution.py:34
  58.0 528.4 %while.14 = (s32[]{:T(128)}, f32[4,262144]{1,0:T(4,128)}, f32[4,262144]{1,0:T(4,128)}, f32[262144]{0:T(1024)S(1)}, f32[]{:T(128)}, /*index=5*/f32[]{:T(128)}, s32[]{:T(128)}) while((s32[]{:T(128)}, f32[4,262144]{1,0:T(4,128)}, f32[4,262144]{1,0:T(4,128)}, f32[262144]{0:T(1024)S(1)}, f32[]{:T(128)}, /*index=5*/f32[]{:T(128)}, s32[]{:T(128)}) %tuple.84), condition=%wide.region_1.2_spmd, body=%wide.region_0.1_spmd.sunk | while | flops 28311552 | bytes 190840976 | solution.py:41
  58.3 4.6 copy.33
  72.4 4.5 fusion.85
  81.5 20.9 %divide_subtract_fusion.2 = f32[4,262144]{1,0:T(4,128)S(1)} fusion(f32[4,262144]{1,0:T(4,128)S(1)} %copy-done.3, f32[4,262144]{1,0:T(4,128)S(1)} %copy-done, f32[4,1]{1,0:T(4,128)S(1)} %get-tuple-element.222, f32[4,262143]{1,0:T(4,128)} %get-tuple-element.223, f32[4,262081]{1,0:T(4,128)} %get-tuple-element.224, f32[4,63]{1,0:T(4,128)S(1)} %get-tuple-element.225, ...), kind=kLoop, calls=%fused_computation.clone.1 | loop fusion | flops 23068672 | bytes 43515912 | tf_op jit(solution)/shard_map/while/body/eval_jaxpr/sub | solution.py:38
  106.3 4.6 copy.33
  120.4 4.5 fusion.85
  129.5 20.9 %divide_subtract_fusion.2 = f32[4,262144]{1,0:T(4,128)S(1)} fusion(f32[4,262144]{1,0:T(4,128)S(1)} %copy-done.3, f32[4,262144]{1,0:T(4,128)S(1)} %copy-done, f32[4,1]{1,0:T(4,128)S(1)} %get-tuple-element.222, f32[4,262143]{1,0:T(4,128)} %get-tuple-element.223, f32[4,262081]{1,0:T(4,128)} %get-tuple-element.224, f32[4,63]{1,0:T(4,128)S(1)} %get-tuple-element.225, ...), kind=kLoop, calls=%fused_computation.clone.1 | loop fusion | flops 23068672 | bytes 43515912 | tf_op jit(solution)/shard_map/while/body/eval_jaxpr/sub | solution.py:38
  154.3 4.6 copy.33
  168.4 4.5 fusion.85
  177.5 20.9 %divide_subtract_fusion.2 = f32[4,262144]{1,0:T(4,128)S(1)} fusion(f32[4,262144]{1,0:T(4,128)S(1)} %copy-done.3, f32[4,262144]{1,0:T(4,128)S(1)} %copy-done, f32[4,1]{1,0:T(4,128)S(1)} %get-tuple-element.222, f32[4,262143]{1,0:T(4,128)} %get-tuple-element.223, f32[4,262081]{1,0:T(4,128)} %get-tuple-element.224, f32[4,63]{1,0:T(4,128)S(1)} %get-tuple-element.225, ...), kind=kLoop, calls=%fused_computation.clone.1 | loop fusion | flops 23068672 | bytes 43515912 | tf_op jit(solution)/shard_map/while/body/eval_jaxpr/sub | solution.py:38
  202.3 4.6 copy.33
  225.5 20.9 %divide_subtract_fusion.2 = f32[4,262144]{1,0:T(4,128)S(1)} fusion(f32[4,262144]{1,0:T(4,128)S(1)} %copy-done.3, f32[4,262144]{1,0:T(4,128)S(1)} %copy-done, f32[4,1]{1,0:T(4,128)S(1)} %get-tuple-element.222, f32[4,262143]{1,0:T(4,128)} %get-tuple-element.223, f32[4,262081]{1,0:T(4,128)} %get-tuple-element.224, f32[4,63]{1,0:T(4,128)S(1)} %get-tuple-element.225, ...), kind=kLoop, calls=%fused_computation.clone.1 | loop fusion | flops 23068672 | bytes 43515912 | tf_op jit(solution)/shard_map/while/body/eval_jaxpr/sub | solution.py:38
  250.3 4.6 copy.33
  273.5 20.9 %divide_subtract_fusion.2 = f32[4,262144]{1,0:T(4,128)S(1)} fusion(f32[4,262144]{1,0:T(4,128)S(1)} %copy-done.3, f32[4,262144]{1,0:T(4,128)S(1)} %copy-done, f32[4,1]{1,0:T(4,128)S(1)} %get-tuple-element.222, f32[4,262143]{1,0:T(4,128)} %get-tuple-element.223, f32[4,262081]{1,0:T(4,128)} %get-tuple-element.224, f32[4,63]{1,0:T(4,128)S(1)} %get-tuple-element.225, ...), kind=kLoop, calls=%fused_computation.clone.1 | loop fusion | flops 23068672 | bytes 43515912 | tf_op jit(solution)/shard_map/while/body/eval_jaxpr/sub | solution.py:38
  298.3 4.6 copy.33
  321.4 20.9 %divide_subtract_fusion.2 = f32[4,262144]{1,0:T(4,128)S(1)} fusion(f32[4,262144]{1,0:T(4,128)S(1)} %copy-done.3, f32[4,262144]{1,0:T(4,128)S(1)} %copy-done, f32[4,1]{1,0:T(4,128)S(1)} %get-tuple-element.222, f32[4,262143]{1,0:T(4,128)} %get-tuple-element.223, f32[4,262081]{1,0:T(4,128)} %get-tuple-element.224, f32[4,63]{1,0:T(4,128)S(1)} %get-tuple-element.225, ...), kind=kLoop, calls=%fused_computation.clone.1 | loop fusion | flops 23068672 | bytes 43515912 | tf_op jit(solution)/shard_map/while/body/eval_jaxpr/sub | solution.py:38
  346.3 4.6 copy.33
  360.3 4.5 fusion.85
  369.4 20.9 %divide_subtract_fusion.2 = f32[4,262144]{1,0:T(4,128)S(1)} fusion(f32[4,262144]{1,0:T(4,128)S(1)} %copy-done.3, f32[4,262144]{1,0:T(4,128)S(1)} %copy-done, f32[4,1]{1,0:T(4,128)S(1)} %get-tuple-element.222, f32[4,262143]{1,0:T(4,128)} %get-tuple-element.223, f32[4,262081]{1,0:T(4,128)} %get-tuple-element.224, f32[4,63]{1,0:T(4,128)S(1)} %get-tuple-element.225, ...), kind=kLoop, calls=%fused_computation.clone.1 | loop fusion | flops 23068672 | bytes 43515912 | tf_op jit(solution)/shard_map/while/body/eval_jaxpr/sub | solution.py:38
  394.2 4.6 copy.33
  408.3 4.5 fusion.85
  417.4 20.9 %divide_subtract_fusion.2 = f32[4,262144]{1,0:T(4,128)S(1)} fusion(f32[4,262144]{1,0:T(4,128)S(1)} %copy-done.3, f32[4,262144]{1,0:T(4,128)S(1)} %copy-done, f32[4,1]{1,0:T(4,128)S(1)} %get-tuple-element.222, f32[4,262143]{1,0:T(4,128)} %get-tuple-element.223, f32[4,262081]{1,0:T(4,128)} %get-tuple-element.224, f32[4,63]{1,0:T(4,128)S(1)} %get-tuple-element.225, ...), kind=kLoop, calls=%fused_computation.clone.1 | loop fusion | flops 23068672 | bytes 43515912 | tf_op jit(solution)/shard_map/while/body/eval_jaxpr/sub | solution.py:38
  442.2 4.6 copy.33
  456.3 4.5 fusion.85
  465.4 20.9 %divide_subtract_fusion.2 = f32[4,262144]{1,0:T(4,128)S(1)} fusion(f32[4,262144]{1,0:T(4,128)S(1)} %copy-done.3, f32[4,262144]{1,0:T(4,128)S(1)} %copy-done, f32[4,1]{1,0:T(4,128)S(1)} %get-tuple-element.222, f32[4,262143]{1,0:T(4,128)} %get-tuple-element.223, f32[4,262081]{1,0:T(4,128)} %get-tuple-element.224, f32[4,63]{1,0:T(4,128)S(1)} %get-tuple-element.225, ...), kind=kLoop, calls=%fused_computation.clone.1 | loop fusion | flops 23068672 | bytes 43515912 | tf_op jit(solution)/shard_map/while/body/eval_jaxpr/sub | solution.py:38
  490.2 4.6 copy.33
  513.4 20.9 %divide_subtract_fusion.2 = f32[4,262144]{1,0:T(4,128)S(1)} fusion(f32[4,262144]{1,0:T(4,128)S(1)} %copy-done.3, f32[4,262144]{1,0:T(4,128)S(1)} %copy-done, f32[4,1]{1,0:T(4,128)S(1)} %get-tuple-element.222, f32[4,262143]{1,0:T(4,128)} %get-tuple-element.223, f32[4,262081]{1,0:T(4,128)} %get-tuple-element.224, f32[4,63]{1,0:T(4,128)S(1)} %get-tuple-element.225, ...), kind=kLoop, calls=%fused_computation.clone.1 | loop fusion | flops 23068672 | bytes 43515912 | tf_op jit(solution)/shard_map/while/body/eval_jaxpr/sub | solution.py:38
  538.2 4.6 copy.33
  561.4 20.9 %divide_subtract_fusion.2 = f32[4,262144]{1,0:T(4,128)S(1)} fusion(f32[4,262144]{1,0:T(4,128)S(1)} %copy-done.3, f32[4,262144]{1,0:T(4,128)S(1)} %copy-done, f32[4,1]{1,0:T(4,128)S(1)} %get-tuple-element.222, f32[4,262143]{1,0:T(4,128)} %get-tuple-element.223, f32[4,262081]{1,0:T(4,128)} %get-tuple-element.224, f32[4,63]{1,0:T(4,128)S(1)} %get-tuple-element.225, ...), kind=kLoop, calls=%fused_computation.clone.1 | loop fusion | flops 23068672 | bytes 43515912 | tf_op jit(solution)/shard_map/while/body/eval_jaxpr/sub | solution.py:38
  586.3 4.6 copy.29
  593.1 4.5 fusion.45
  597.7 4.5 fusion.48
  609.9 23.3 %fusion.27 = f32[4,262144]{1,0:T(4,128)S(1)} fusion(f32[4,262144]{1,0:T(4,128)S(1)} %bitcast.66, f32[4,258048]{1,0:T(4,128)} %get-tuple-element.142, f32[4,4096]{1,0:T(4,128)S(1)} %get-tuple-element.144, f32[4,4096]{1,0:T(4,128)S(1)} %get-tuple-element.143, f32[4,258048]{1,0:T(4,128)} %get-tuple-element.141, f32[4,63]{1,0:T(4,128)S(1)} %get-tuple-element.138, ...), kind=kLoop, calls=%fused_computation.44 | loop fusion | flops 17825792 | bytes 39321600 | tf_op jit(solution)/shard_map/add | solution.py:28
  633.2 101.2 %all_to_all.38 = f32[4,32,8192]{2,0,1:T(4,128)} all-to-all(f32[4,32,8192]{2,0,1:T(4,128)S(1)} %bitcast.67), channel_id=1, replica_groups=mesh['ob'=8,'pt'=4] {'ob','pt'}, dimensions={1} | all-to-all | bytes 8388608 | tf_op jit(solution)/shard_map/all_to_all | solution.py:54
  738.0 5.5 all_to_all.35
  743.6 88.6 %all-to-all-done = f32[4,32,8192]{2,0,1:T(4,128)} async-done(((f32[4,32,8192]{2,0,1:T(4,128)}), f32[4,32,8192]{2,0,1:T(4,128)}, u32[]{:S(2)}, u32[]{:S(2)}) %all-to-all-start) | async-done | bytes 4194336 | tf_op jit(solution)/shard_map/all_to_all | solution.py:53
  832.1 5.3 all_to_all.31
  837.4 7.7 convolution_multiply_fusion.1
  849.3 9.9 convolution_bitcast_fusion.1
  859.1 5.6 copy.17
  864.7 110.7 %all-reduce.6.cloned.1.call-done = (f32[128,128]{1,0:T(8,128)}, f32[128,128]{1,0:T(8,128)}) async-done(((f32[128,128]{1,0:T(8,128)}, f32[128,128]{1,0:T(8,128)}), (f32[128,128]{1,0:T(8,128)}, f32[128,128]{1,0:T(8,128)})) %all-reduce.6.cloned.1.call-update) | async-done | bytes 131088
  977.1 39.6 %all-reduce.2 = (f32[128]{0:T(128)S(1)}, f32[128]{0:T(128)S(1)}) all-reduce(f32[128]{0:T(128)S(1)} %fusion.30, f32[128]{0:T(128)S(1)} %fusion.31), channel_id=1, replica_groups=mesh['ob'=8,'pt'=4] {'ob','pt'}, use_global_device_ids=true, to_apply=%region_5.6 | all-reduce | flops 256 | bytes 2048 | tf_op jit(solution)/shard_map/psum | solution.py:68
  1016.7 10.5 %fusion.13 = f32[128,8192]{0,1:T(8,128)} fusion(f32[128,8192]{1,0:T(8,128)} %all_to_all.35, f32[128,128]{1,0:T(8,128)S(1)} %copy-done.12, f32[128,8192]{0,1:T(8,128)} %convolution_bitcast_fusion.1, f32[128]{0:T(128)S(1)} %add_divide_fusion), kind=kOutput, calls=%fused_computation.22 | convolution fusion | flops 1612709888 | bytes 12648960 | tf_op jit(solution)/shard_map/dot_general | solution.py:63
  1027.2 5.6 copy.18
  (236 shorter events, 250.9 us)
Async XLA Ops:
  9.4 16.8 %copy-start.2 = (f32[4,262144]{1,0:T(4,128)}, f32[4,262144]{1,0:T(4,128)S(1)}, u32[]{:S(2)}) copy-start(f32[4,262144]{1,0:T(4,128)S(1)} %copy.48) | copy-start | bytes 12582916
  26.6 6.7 copy-start.8
  26.6 6.7 copy-start.10
  28.6 4.7 copy-start.5
  65.9 2.7 copy-start
  76.9 4.6 copy-start.3
  113.9 2.7 copy-start
  124.8 4.6 copy-start.3
  161.9 2.7 copy-start
  172.8 4.6 copy-start.3
  209.9 2.7 copy-start
  220.8 4.6 copy-start.3
  257.9 2.7 copy-start
  268.8 4.6 copy-start.3
  305.9 2.7 copy-start
  316.8 4.6 copy-start.3
  353.9 2.7 copy-start
  364.8 4.6 copy-start.3
  401.8 2.7 copy-start
  412.8 4.6 copy-start.3
  449.8 2.7 copy-start
  460.7 4.6 copy-start.3
  497.8 2.7 copy-start
  508.7 4.6 copy-start.3
  545.8 2.7 copy-start
  556.7 4.6 copy-start.3
  591.0 2.2 copy-start.1
  607.1 2.7 copy-start.7
  607.1 2.7 copy-start.9
  607.1 2.7 copy-start.11
  734.4 97.7 %all-to-all-start = ((f32[4,32,8192]{2,0,1:T(4,128)}), f32[4,32,8192]{2,0,1:T(4,128)}, u32[]{:S(2)}, u32[]{:S(2)}) async-start(f32[4,32,8192]{2,0,1:T(4,128)} %bitcast.55), calls=%async_computation | async-start | bytes 8388608 | tf_op jit(solution)/shard_map/all_to_all | solution.py:53
  738.0 237.4 %all-reduce.6.cloned.1.call-start = ((), (), s32[]{:S(2)}) async-start(), calls=%async_computation.2 | async-start | bytes 262144
  837.4 7.7 copy-start.4
  837.4 7.7 copy-start.6
  845.1 4.1 copy-start.12
  976.1 51.1 %copy-start.13 = (f32[4,128]{1,0:T(4,128)}, f32[4,128]{1,0:T(4,128)S(1)}, u32[]{:S(2)}) copy-start(f32[4,128]{1,0:T(4,128)S(1)} %constant_dynamic-slice_fusion) | copy-start | bytes 6148
  976.8 50.5 %copy-start.14 = (f32[4,128]{1,0:T(4,128)}, f32[4,128]{1,0:T(4,128)S(1)}, u32[]{:S(2)}) copy-start(f32[4,128]{1,0:T(4,128)S(1)} %constant_dynamic-slice_fusion.1) | copy-start | bytes 6148
  1016.7 10.5 %copy-start.15 = (f32[128]{0:T(128)}, f32[128]{0:T(128)S(1)}, u32[]{:S(2)}) copy-start(f32[128]{0:T(128)S(1)} %add_divide_fusion) | copy-start | bytes 1540
Sparse Core Ops, SparseCore 0:
  849.4 125.9 all-reduce.5
where the time goes:
time: 1040 us
  local copies, waits for them, and re-layouts  349 us (34%)
  other arithmetic  299 us (29%)
  waiting for transfers between devices  199 us (19%)
  blocking collectives  141 us (14%)
  matrix products  32.6 us (3%)
  between operations  15.2 us (1%)
    sub x11, other arithmetic, advance(): 2.0 * (apply_ham(present, potential) - center * present) / half_width  229 us
    while x88, local copies, waits for them, and re-layouts  124 us
    unnamed x2, waiting for transfers between devices  111 us
    all_to_all x1, blocking collectives, on_device(): lax.all_to_all(applied, ('ob', 'pt'), split_axis=1, concat_axis=0, tiled=...  101 us
    all_to_all x1, waiting for transfers between devices, on_device(): lax.all_to_all(filtered, ('ob', 'pt'), split_axis=1, concat_axis=0, tiled...  88.6 us
    slice x24, local copies, waits for them, and re-layouts, apply_ham(): jnp.roll(fields, 1 - G, axis=-1)  54.5 us
    slice x24, local copies, waits for them, and re-layouts, apply_ham(): jnp.roll(fields, plane_len, axis=-1) + jnp.roll(fields, -plane_len, axis=-1)  49.1 us
    slice x24, local copies, waits for them, and re-layouts, apply_ham(): jnp.roll(fields, 1, axis=-1)  46.4 us
  transfers between devices with their start and end apart: 2, of which 2 were waited for; matrix products, arithmetic and copies ran while one was open for 1% of the time, Pallas kernels for 0%

commit v1 on v0

--- a/solution.py
+++ b/solution.py
@@ -8,6 +8,12 @@
 NPTS = 262144
 upper_bound = 8.0
 quot_eps = 1e-06
+
+
+def stacked_exchange(x, axis, split, join):
+    cells = jnp.split(x, lax.axis_size(axis), axis=split)
+    received = lax.all_to_all(jnp.stack(cells), axis, 0, 0)
+    return jnp.concatenate(received, axis=join)
 
 
 def apply_ham(fields, potential):
@@ -51,7 +57,7 @@
     per_dev = total_orb // (n_ob * n_pt)
     rows_filt, rows_appl = (
         lax.all_to_all(filtered, ("ob", "pt"), split_axis=1, concat_axis=0, tiled=True),
-        lax.all_to_all(applied, ("ob", "pt"), split_axis=1, concat_axis=0, tiled=True),
+        stacked_exchange(applied, ("ob", "pt"), 1, 0),
     )
     part_gram = jnp.dot(rows_filt, rows_filt.T, precision=high) / NPTS
     part_hamil = jnp.dot(rows_filt, rows_appl.T, precision=high) / NPTS

time: 1040 us -> 997 us (0.959)
  blocking collectives: 141 us -> 39.5 us
  local copies, waits for them, and re-layouts: 349 us -> 370 us
  waiting for transfers between devices: 199 us -> 218 us
    all_to_all x1 -> x0, blocking collectives: 101 us -> none  [on_device(): lax.all_to_all(applied, ('ob', 'pt'), split_axis=1, concat_axis=0, tiled=...]
    all_to_all x0 -> x1, waiting for transfers between devices: none -> 81 us  [stacked_exchange(): received = lax.all_to_all(jnp.stack(cells), axis, 0, 0)]
    all_to_all x1, waiting for transfers between devices: 88.6 us -> 26.1 us  [on_device(): lax.all_to_all(filtered, ('ob', 'pt'), split_axis=1, concat_axis=0, tiled...]
    unnamed x37 -> x64, local copies, waits for them, and re-layouts: 29.7 us -> 50.3 us
  transfers between devices with their start and end apart: 2 -> 3, of which waited for: 2 -> 3; matrix products, arithmetic and copies ran while one was open for 1% -> 9% of each run, Pallas kernels for 0% -> 0%
where the time goes in v1:
time: 997 us; the launch traced here: 992 us
  local copies, waits for them, and re-layouts  370 us (37%)
  other arithmetic  299 us (30%)
  waiting for transfers between devices  218 us (22%)
  blocking collectives  39.5 us (4%)
  matrix products  35.9 us (4%)
  between operations  15.2 us (2%)
  starting transfers between devices  13.5 us (1%)
    sub x11, other arithmetic, advance(): 2.0 * (apply_ham(present, potential) - center * present) / half_width  229 us
    while x88, local copies, waits for them, and re-layouts  124 us
    unnamed x2, waiting for transfers between devices  111 us
    all_to_all x1, waiting for transfers between devices, stacked_exchange(): received = lax.all_to_all(jnp.stack(cells), axis, 0, 0)  81 us
    slice x24, local copies, waits for them, and re-layouts, apply_ham(): jnp.roll(fields, 1 - G, axis=-1)  54.5 us
    unnamed x64, local copies, waits for them, and re-layouts  50.3 us
    slice x24, local copies, waits for them, and re-layouts, apply_ham(): jnp.roll(fields, plane_len, axis=-1) + jnp.roll(fields, -plane_len, axis=-1)  49.1 us
    slice x24, local copies, waits for them, and re-layouts, apply_ham(): jnp.roll(fields, 1, axis=-1)  46.4 us
  transfers between devices with their start and end apart: 3, of which 3 were waited for; matrix products, arithmetic and copies ran while one was open for 9% of the time, Pallas kernels for 0%

profile of v1, /device:TPU:0, one launch (start us, length us, event | category | flops | bytes accessed | tf_op | source)
XLA Modules:
  0.0 991.9 jit_solution(12467556831801859708)
XLA Ops:
  13.5 4.6 fusion.89
  18.1 4.5 fusion.92
  28.6 4.7 copy.20
  33.3 24.7 %fusion.29 = f32[4,262144]{1,0:T(4,128)} fusion(f32[4,262144]{1,0:T(4,128)} %copy-done.2, f32[4,1]{1,0:T(4,128)S(1)} %get-tuple-element.162, f32[4,262143]{1,0:T(4,128)} %get-tuple-element.164, f32[4,262081]{1,0:T(4,128)} %get-tuple-element.158, f32[4,63]{1,0:T(4,128)S(1)} %get-tuple-element.160, f32[4,262143]{1,0:T(4,128)} %get-tuple-element.163, ...), kind=kLoop, calls=%fused_computation.49 | loop fusion | flops 20971520 | bytes 39321608 | tf_op jit(solution)/shard_map/div | solution.py:40
  58.0 528.4 %while.14 = (s32[]{:T(128)}, f32[4,262144]{1,0:T(4,128)}, f32[4,262144]{1,0:T(4,128)}, f32[262144]{0:T(1024)S(1)}, f32[]{:T(128)}, /*index=5*/f32[]{:T(128)}, s32[]{:T(128)}) while((s32[]{:T(128)}, f32[4,262144]{1,0:T(4,128)}, f32[4,262144]{1,0:T(4,128)}, f32[262144]{0:T(1024)S(1)}, f32[]{:T(128)}, /*index=5*/f32[]{:T(128)}, s32[]{:T(128)}) %tuple.84), condition=%wide.region_1.2_spmd, body=%wide.region_0.1_spmd.sunk | while | flops 28311552 | bytes 190840976 | solution.py:47
  58.3 4.6 copy.31
  72.4 4.5 fusion.117
  81.5 20.9 %divide_subtract_fusion.2 = f32[4,262144]{1,0:T(4,128)S(1)} fusion(f32[4,262144]{1,0:T(4,128)S(1)} %copy-done.3, f32[4,262144]{1,0:T(4,128)S(1)} %copy-done, f32[4,1]{1,0:T(4,128)S(1)} %get-tuple-element.222, f32[4,262143]{1,0:T(4,128)} %get-tuple-element.223, f32[4,262081]{1,0:T(4,128)} %get-tuple-element.224, f32[4,63]{1,0:T(4,128)S(1)} %get-tuple-element.225, ...), kind=kLoop, calls=%fused_computation.clone.1 | loop fusion | flops 23068672 | bytes 43515912 | tf_op jit(solution)/shard_map/while/body/eval_jaxpr/sub | solution.py:44
  106.3 4.6 copy.31
  120.4 4.5 fusion.117
  129.5 20.9 %divide_subtract_fusion.2 = f32[4,262144]{1,0:T(4,128)S(1)} fusion(f32[4,262144]{1,0:T(4,128)S(1)} %copy-done.3, f32[4,262144]{1,0:T(4,128)S(1)} %copy-done, f32[4,1]{1,0:T(4,128)S(1)} %get-tuple-element.222, f32[4,262143]{1,0:T(4,128)} %get-tuple-element.223, f32[4,262081]{1,0:T(4,128)} %get-tuple-element.224, f32[4,63]{1,0:T(4,128)S(1)} %get-tuple-element.225, ...), kind=kLoop, calls=%fused_computation.clone.1 | loop fusion | flops 23068672 | bytes 43515912 | tf_op jit(solution)/shard_map/while/body/eval_jaxpr/sub | solution.py:44
  154.3 4.6 copy.31
  177.5 20.9 %divide_subtract_fusion.2 = f32[4,262144]{1,0:T(4,128)S(1)} fusion(f32[4,262144]{1,0:T(4,128)S(1)} %copy-done.3, f32[4,262144]{1,0:T(4,128)S(1)} %copy-done, f32[4,1]{1,0:T(4,128)S(1)} %get-tuple-element.222, f32[4,262143]{1,0:T(4,128)} %get-tuple-element.223, f32[4,262081]{1,0:T(4,128)} %get-tuple-element.224, f32[4,63]{1,0:T(4,128)S(1)} %get-tuple-element.225, ...), kind=kLoop, calls=%fused_computation.clone.1 | loop fusion | flops 23068672 | bytes 43515912 | tf_op jit(solution)/shard_map/while/body/eval_jaxpr/sub | solution.py:44
  202.3 4.6 copy.31
  225.5 20.9 %divide_subtract_fusion.2 = f32[4,262144]{1,0:T(4,128)S(1)} fusion(f32[4,262144]{1,0:T(4,128)S(1)} %copy-done.3, f32[4,262144]{1,0:T(4,128)S(1)} %copy-done, f32[4,1]{1,0:T(4,128)S(1)} %get-tuple-element.222, f32[4,262143]{1,0:T(4,128)} %get-tuple-element.223, f32[4,262081]{1,0:T(4,128)} %get-tuple-element.224, f32[4,63]{1,0:T(4,128)S(1)} %get-tuple-element.225, ...), kind=kLoop, calls=%fused_computation.clone.1 | loop fusion | flops 23068672 | bytes 43515912 | tf_op jit(solution)/shard_map/while/body/eval_jaxpr/sub | solution.py:44
  250.3 4.6 copy.31
  273.5 20.9 %divide_subtract_fusion.2 = f32[4,262144]{1,0:T(4,128)S(1)} fusion(f32[4,262144]{1,0:T(4,128)S(1)} %copy-done.3, f32[4,262144]{1,0:T(4,128)S(1)} %copy-done, f32[4,1]{1,0:T(4,128)S(1)} %get-tuple-element.222, f32[4,262143]{1,0:T(4,128)} %get-tuple-element.223, f32[4,262081]{1,0:T(4,128)} %get-tuple-element.224, f32[4,63]{1,0:T(4,128)S(1)} %get-tuple-element.225, ...), kind=kLoop, calls=%fused_computation.clone.1 | loop fusion | flops 23068672 | bytes 43515912 | tf_op jit(solution)/shard_map/while/body/eval_jaxpr/sub | solution.py:44
  298.3 4.6 copy.31
  321.4 20.9 %divide_subtract_fusion.2 = f32[4,262144]{1,0:T(4,128)S(1)} fusion(f32[4,262144]{1,0:T(4,128)S(1)} %copy-done.3, f32[4,262144]{1,0:T(4,128)S(1)} %copy-done, f32[4,1]{1,0:T(4,128)S(1)} %get-tuple-element.222, f32[4,262143]{1,0:T(4,128)} %get-tuple-element.223, f32[4,262081]{1,0:T(4,128)} %get-tuple-element.224, f32[4,63]{1,0:T(4,128)S(1)} %get-tuple-element.225, ...), kind=kLoop, calls=%fused_computation.clone.1 | loop fusion | flops 23068672 | bytes 43515912 | tf_op jit(solution)/shard_map/while/body/eval_jaxpr/sub | solution.py:44
  346.3 4.6 copy.31
  360.3 4.5 fusion.117
  369.4 20.9 %divide_subtract_fusion.2 = f32[4,262144]{1,0:T(4,128)S(1)} fusion(f32[4,262144]{1,0:T(4,128)S(1)} %copy-done.3, f32[4,262144]{1,0:T(4,128)S(1)} %copy-done, f32[4,1]{1,0:T(4,128)S(1)} %get-tuple-element.222, f32[4,262143]{1,0:T(4,128)} %get-tuple-element.223, f32[4,262081]{1,0:T(4,128)} %get-tuple-element.224, f32[4,63]{1,0:T(4,128)S(1)} %get-tuple-element.225, ...), kind=kLoop, calls=%fused_computation.clone.1 | loop fusion | flops 23068672 | bytes 43515912 | tf_op jit(solution)/shard_map/while/body/eval_jaxpr/sub | solution.py:44
  394.2 4.6 copy.31
  408.3 4.5 fusion.117
  417.4 20.9 %divide_subtract_fusion.2 = f32[4,262144]{1,0:T(4,128)S(1)} fusion(f32[4,262144]{1,0:T(4,128)S(1)} %copy-done.3, f32[4,262144]{1,0:T(4,128)S(1)} %copy-done, f32[4,1]{1,0:T(4,128)S(1)} %get-tuple-element.222, f32[4,262143]{1,0:T(4,128)} %get-tuple-element.223, f32[4,262081]{1,0:T(4,128)} %get-tuple-element.224, f32[4,63]{1,0:T(4,128)S(1)} %get-tuple-element.225, ...), kind=kLoop, calls=%fused_computation.clone.1 | loop fusion | flops 23068672 | bytes 43515912 | tf_op jit(solution)/shard_map/while/body/eval_jaxpr/sub | solution.py:44
  442.2 4.6 copy.31
  465.4 20.9 %divide_subtract_fusion.2 = f32[4,262144]{1,0:T(4,128)S(1)} fusion(f32[4,262144]{1,0:T(4,128)S(1)} %copy-done.3, f32[4,262144]{1,0:T(4,128)S(1)} %copy-done, f32[4,1]{1,0:T(4,128)S(1)} %get-tuple-element.222, f32[4,262143]{1,0:T(4,128)} %get-tuple-element.223, f32[4,262081]{1,0:T(4,128)} %get-tuple-element.224, f32[4,63]{1,0:T(4,128)S(1)} %get-tuple-element.225, ...), kind=kLoop, calls=%fused_computation.clone.1 | loop fusion | flops 23068672 | bytes 43515912 | tf_op jit(solution)/shard_map/while/body/eval_jaxpr/sub | solution.py:44
  490.2 4.6 copy.31
  513.4 20.9 %divide_subtract_fusion.2 = f32[4,262144]{1,0:T(4,128)S(1)} fusion(f32[4,262144]{1,0:T(4,128)S(1)} %copy-done.3, f32[4,262144]{1,0:T(4,128)S(1)} %copy-done, f32[4,1]{1,0:T(4,128)S(1)} %get-tuple-element.222, f32[4,262143]{1,0:T(4,128)} %get-tuple-element.223, f32[4,262081]{1,0:T(4,128)} %get-tuple-element.224, f32[4,63]{1,0:T(4,128)S(1)} %get-tuple-element.225, ...), kind=kLoop, calls=%fused_computation.clone.1 | loop fusion | flops 23068672 | bytes 43515912 | tf_op jit(solution)/shard_map/while/body/eval_jaxpr/sub | solution.py:44
  538.2 4.6 copy.31
  561.4 20.9 %divide_subtract_fusion.2 = f32[4,262144]{1,0:T(4,128)S(1)} fusion(f32[4,262144]{1,0:T(4,128)S(1)} %copy-done.3, f32[4,262144]{1,0:T(4,128)S(1)} %copy-done, f32[4,1]{1,0:T(4,128)S(1)} %get-tuple-element.222, f32[4,262143]{1,0:T(4,128)} %get-tuple-element.223, f32[4,262081]{1,0:T(4,128)} %get-tuple-element.224, f32[4,63]{1,0:T(4,128)S(1)} %get-tuple-element.225, ...), kind=kLoop, calls=%fused_computation.clone.1 | loop fusion | flops 23068672 | bytes 43515912 | tf_op jit(solution)/shard_map/while/body/eval_jaxpr/sub | solution.py:44
  586.3 7.5 all-to-all-start
  593.8 4.6 copy.27
  605.1 4.5 fusion.80
  617.3 23.3 %fusion.27 = f32[4,262144]{1,0:T(4,128)S(1)} fusion(f32[4,262144]{1,0:T(4,128)S(1)} %bitcast.191, f32[4,258048]{1,0:T(4,128)} %get-tuple-element.142, f32[4,4096]{1,0:T(4,128)S(1)} %get-tuple-element.144, f32[4,4096]{1,0:T(4,128)S(1)} %get-tuple-element.143, f32[4,258048]{1,0:T(4,128)} %get-tuple-element.141, f32[4,63]{1,0:T(4,128)S(1)} %get-tuple-element.138, ...), kind=kLoop, calls=%fused_computation.44 | loop fusion | flops 17825792 | bytes 39321600 | tf_op jit(solution)/shard_map/add | solution.py:34
  661.9 26.1 %all-to-all-done = f32[4,32,8192]{2,0,1:T(4,128)} async-done(((f32[4,32,8192]{2,0,1:T(4,128)}), f32[4,32,8192]{2,0,1:T(4,128)}, u32[]{:S(2)}, u32[]{:S(2)}) %all-to-all-start) | async-done | bytes 4194336 | tf_op jit(solution)/shard_map/all_to_all | solution.py:59
  688.0 6.0 all-to-all-start.1
  694.0 5.5 all_to_all.20
  699.5 7.6 convolution_multiply_fusion.1
  707.1 81.0 %all-to-all-done.1 = f32[32,4,8192]{2,1,0:T(4,128)} async-done(((f32[32,4,8192]{2,1,0:T(4,128)}), f32[32,4,8192]{2,1,0:T(4,128)}, u32[]{:S(2)}, u32[]{:S(2)}) %all-to-all-start.1) | async-done | bytes 4194336 | tf_op jit(solution)/shard_map/all_to_all | solution.py:15
  788.2 5.3 reshape.99
  793.5 7.6 convolution_multiply_fusion
  801.1 9.9 convolution_bitcast_fusion.1
  811.0 5.6 copy.15
  816.6 110.8 %all-reduce.6.cloned.1.call-done = (f32[128,128]{1,0:T(8,128)}, f32[128,128]{1,0:T(8,128)}) async-done(((f32[128,128]{1,0:T(8,128)}, f32[128,128]{1,0:T(8,128)}), (f32[128,128]{1,0:T(8,128)}, f32[128,128]{1,0:T(8,128)})) %all-reduce.6.cloned.1.call-update) | async-done | bytes 131088
  929.1 39.5 %all-reduce.2 = (f32[128]{0:T(128)S(1)}, f32[128]{0:T(128)S(1)}) all-reduce(f32[128]{0:T(128)S(1)} %fusion.30, f32[128]{0:T(128)S(1)} %fusion.31), channel_id=1, replica_groups=mesh['ob'=8,'pt'=4] {'ob','pt'}, use_global_device_ids=true, to_apply=%region_5.6 | all-reduce | flops 256 | bytes 2048 | tf_op jit(solution)/shard_map/psum | solution.py:74
  968.6 10.5 %fusion.13 = f32[128,8192]{0,1:T(8,128)} fusion(f32[128,8192]{1,0:T(8,128)} %reshape.99, f32[128,128]{1,0:T(8,128)S(1)} %copy-done.10, f32[128,8192]{0,1:T(8,128)} %convolution_bitcast_fusion.1, f32[128]{0:T(128)S(1)} %add_divide_fusion), kind=kOutput, calls=%fused_computation.22 | convolution fusion | flops 1612709888 | bytes 12648960 | tf_op jit(solution)/shard_map/dot_general | solution.py:69
  979.2 5.6 copy.16
  (265 shorter events, 277.8 us)
Async XLA Ops:
  9.4 16.8 %copy-start.2 = (f32[4,262144]{1,0:T(4,128)}, f32[4,262144]{1,0:T(4,128)S(1)}, u32[]{:S(2)}) copy-start(f32[4,262144]{1,0:T(4,128)S(1)} %copy.77) | copy-start | bytes 12582916
  26.6 6.7 copy-start.6
  26.6 6.7 copy-start.8
  28.6 4.7 copy-start.4
  65.9 2.7 copy-start
  76.9 4.6 copy-start.3
  113.9 2.7 copy-start
  124.8 4.6 copy-start.3
  161.9 2.7 copy-start
  172.8 4.6 copy-start.3
  209.9 2.7 copy-start
  220.8 4.6 copy-start.3
  257.9 2.7 copy-start
  268.8 4.6 copy-start.3
  305.9 2.7 copy-start
  316.8 4.6 copy-start.3
  353.9 2.7 copy-start
  364.8 4.6 copy-start.3
  401.8 2.7 copy-start
  412.8 4.6 copy-start.3
  449.8 2.7 copy-start
  460.7 4.6 copy-start.3
  497.8 2.7 copy-start
  508.7 4.6 copy-start.3
  545.8 2.7 copy-start
  556.7 4.6 copy-start.3
  586.3 101.6 %all-to-all-start = ((f32[4,32,8192]{2,0,1:T(4,128)}), f32[4,32,8192]{2,0,1:T(4,128)}, u32[]{:S(2)}, u32[]{:S(2)}) async-start(f32[4,32,8192]{2,0,1:T(4,128)} %bitcast.180), calls=%async_computation | async-start | bytes 8388608 | tf_op jit(solution)/shard_map/all_to_all | solution.py:59
  598.5 2.2 copy-start.1
  614.6 2.7 copy-start.5
  614.6 2.7 copy-start.7
  614.6 2.7 copy-start.9
  688.0 100.2 %all-to-all-start.1 = ((f32[32,4,8192]{2,1,0:T(4,128)}), f32[32,4,8192]{2,1,0:T(4,128)}, u32[]{:S(2)}, u32[]{:S(2)}) async-start(f32[32,4,8192]{2,1,0:T(4,128)} %fusion.37), calls=%async_computation.1 | async-start | bytes 8388608 | tf_op jit(solution)/shard_map/all_to_all | solution.py:15
  694.0 233.4 %all-reduce.6.cloned.1.call-start = ((), (), s32[]{:S(2)}) async-start(), calls=%async_computation.2 | async-start | bytes 262144
  793.5 7.6 copy-start.10
  928.0 51.1 %copy-start.11 = (f32[4,128]{1,0:T(4,128)}, f32[4,128]{1,0:T(4,128)S(1)}, u32[]{:S(2)}) copy-start(f32[4,128]{1,0:T(4,128)S(1)} %constant_dynamic-slice_fusion) | copy-start | bytes 6148
  928.7 50.4 %copy-start.12 = (f32[4,128]{1,0:T(4,128)}, f32[4,128]{1,0:T(4,128)S(1)}, u32[]{:S(2)}) copy-start(f32[4,128]{1,0:T(4,128)S(1)} %constant_dynamic-slice_fusion.1) | copy-start | bytes 6148
  968.6 10.5 %copy-start.13 = (f32[128]{0:T(128)}, f32[128]{0:T(128)S(1)}, u32[]{:S(2)}) copy-start(f32[128]{0:T(128)S(1)} %add_divide_fusion) | copy-start | bytes 1540
Sparse Core Ops, SparseCore 0:
  801.2 126.1 all-reduce.5
